TPU v7x, 32 devices: a whole 2x2x4 slice. The times are simulated.
32 devices in a mesh: fsdp: 4 (over z), ctx: 4 (over x, core), tp: 2 (over y).
Axes of the slice: x: 2, y: 2, z: 4, core: 2. Of those that a mesh axis runs over, the one named last changes fastest.
Arguments:
- layer_input: bfloat16 [4, 8, 512, 768], P(None, 'fsdp', 'ctx'), may hold values from -6 to 6
- doc_ids: int32 [4, 8, 512], P(None, 'fsdp', 'ctx'), may hold values from 0 to 3, never falling along the last dimension, each value on 1 to 256 neighbouring positions
- w_qkv: bfloat16 [3, 768, 768], P(None, 'fsdp', 'tp'), may hold values from -0.21875 to 0.21875
- b_qv: float32 [2, 768], P(None, 'tp'), may hold values from -3 to 3
- w_out: bfloat16 [768, 768], P('tp', 'fsdp'), may hold values from -0.625 to 0.625
- b_out: float32 [768], replicated, may hold values from -2 to 2
- ln1_gain: float32 [768], replicated, may hold values from 0.1 to 1.9
- ln1_bias: float32 [768], replicated, may hold values from -2 to 2
- w_up: bfloat16 [768, 3072], P('fsdp', 'tp'), may hold values from -0.21875 to 0.21875
- b_up: float32 [3072], P('tp'), may hold values from -3 to 3
- w_down: bfloat16 [3072, 768], P('tp', 'fsdp'), may hold values from -0.109375 to 0.109375
- b_down: float32 [768], replicated, may hold values from -2 to 2
- ln2_gain: float32 [768], replicated, may hold values from 0.1 to 1.9
- ln2_bias: float32 [768], replicated, may hold values from -2 to 2
- out_grad: bfloat16 [4, 8, 512, 768], P(None, 'fsdp', 'ctx'), may hold values from -6 to 6
Outputs:
- layer_output: bfloat16 [4, 8, 512, 768], P(None, 'fsdp', 'ctx')
- grad_x: bfloat16 [4, 8, 512, 768], P(None, 'fsdp', 'ctx')
- grad_w_qkv: float32 [3, 768, 768], P(None, 'fsdp', 'tp')
- grad_b_qv: float32 [2, 768], P(None, 'tp')
- grad_w_out: float32 [768, 768], P('tp', 'fsdp')
- grad_b_out: float32 [768], replicated
- grad_ln1_gain: float32 [768], replicated
- grad_ln1_bias: float32 [768], replicated
- grad_w_up: float32 [768, 3072], P('fsdp', 'tp')
- grad_b_up: float32 [3072], P('tp')
- grad_w_down: float32 [3072, 768], P('tp', 'fsdp')
- grad_b_down: float32 [768], replicated
- grad_ln2_gain: float32 [768], replicated
- grad_ln2_bias: float32 [768], replicated
Inputs may be any that keep to these rules, and one draw needn't show every extreme that they name: `doc_ids`: within each sequence of 512 tokens the ids never fall and each of the 4 ids marks one run of 1 to 256 tokens.
All inputs are finite; a program needn't handle non-finite values.
Results may differ from a plain program's by a relative error of at most 0.02.
Values may be sent and summed in bfloat16 or wider, within the bound.
No kernel may reach another device: no remote copies, remote signals or barrier semaphores. Data moves between devices by JAX's collectives and lax.ppermute only.
A program may use at most 128 MiB of HBM per device.

v0:
```python
import jax
import jax.numpy as jnp
from jax import lax
from jax.sharding import PartitionSpec as P

HEAD_DIM = 64


def normalize_rows(values_in):
    mean = jnp.mean(values_in, axis=-1, keepdims=True)
    centred = values_in - mean
    var = jnp.mean(centred * centred, axis=-1, keepdims=True)
    scale = lax.rsqrt(var + 1e-12)
    return (centred * scale, scale)


def normalize_back(grad_hat, normed, scale):
    first_mean = jnp.mean(grad_hat, axis=-1, keepdims=True)
    second_mean = jnp.mean(grad_hat * normed, axis=-1, keepdims=True)
    return scale * (grad_hat - first_mean - normed * second_mean)


def collect_weights(weights):
    return (
        lax.all_gather(weights[0], "fsdp", axis=1, tiled=True),
        lax.all_gather(weights[1], "fsdp", axis=1, tiled=True),
        lax.all_gather(weights[2], "fsdp", axis=0, tiled=True),
        lax.all_gather(weights[3], "fsdp", axis=1, tiled=True),
    )


def spread_grads(grads):
    return (
        lax.psum_scatter(
            grads[0].astype(jnp.bfloat16), "fsdp", scatter_dimension=1, tiled=True
        ).astype(jnp.float32),
        lax.psum_scatter(
            grads[1].astype(jnp.bfloat16), "fsdp", scatter_dimension=1, tiled=True
        ).astype(jnp.float32),
        lax.psum_scatter(
            grads[2].astype(jnp.bfloat16), "fsdp", scatter_dimension=0, tiled=True
        ).astype(jnp.float32),
        lax.psum_scatter(
            grads[3].astype(jnp.bfloat16), "fsdp", scatter_dimension=1, tiled=True
        ).astype(jnp.float32),
    )


def attention_probs(query, keys, allowed, log_total):
    scores = jnp.einsum("sqhd,skhd->shqk", query, keys, preferred_element_type=jnp.float32) * 0.125
    masked = jnp.where(allowed, scores, -1e30)
    if log_total is None:
        top = jnp.max(masked, axis=-1, keepdims=True)
        log_total = top + jnp.log(jnp.sum(jnp.exp(masked - top), axis=-1, keepdims=True))
    return (jnp.exp(masked - log_total), log_total)


def body(
    layer_input,
    doc_ids,
    w_qkv,
    b_qv,
    w_out,
    b_out,
    ln1_gain,
    ln1_bias,
    w_up,
    b_up,
    w_down,
    b_down,
    ln2_gain,
    ln2_bias,
    out_grad,
):
    inputs_here, cot_here, ids_here = (layer_input, out_grad, doc_ids)
    key_ids = lax.all_gather(doc_ids, "ctx", axis=2, tiled=True)
    micro, seqs, local_len, width = inputs_here.shape
    full_len = key_ids.shape[2]
    shard_rows = width // lax.axis_size("fsdp")
    local_width = w_qkv.shape[2]
    local_units = w_up.shape[1]
    local_heads = local_width // HEAD_DIM
    rows_count = seqs * local_len
    bias_three = jnp.concatenate(
        [b_qv[0:1], jnp.zeros((1, local_width), jnp.float32), b_qv[1:2]], axis=0
    )[:, None, :]
    local_acc = (
        jnp.zeros((3, width, local_width), jnp.float32),
        jnp.zeros((local_width, width), jnp.float32),
        jnp.zeros((width, local_units), jnp.float32),
        jnp.zeros((local_units, width), jnp.float32),
    )
    shard_acc = (
        jnp.zeros((3, shard_rows, local_width), jnp.float32),
        jnp.zeros((local_width, shard_rows), jnp.float32),
        jnp.zeros((shard_rows, local_units), jnp.float32),
        jnp.zeros((local_units, shard_rows), jnp.float32),
    )
    zero_width = jnp.zeros((width,), jnp.float32)
    grad_bqv = jnp.zeros((2, local_width), jnp.float32)
    grad_bup = jnp.zeros((local_units,), jnp.float32)
    grad_bout, grad_gain1, grad_shift1 = (zero_width, zero_width, zero_width)
    grad_bdown, grad_gain2, grad_shift2 = (zero_width, zero_width, zero_width)
    outputs, input_grads = ([], [])
    for micro_step in range(micro):
        weights_now = collect_weights((w_qkv, w_out, w_up, w_down))
        wq_all, wo_all, wu_all, wd_all = weights_now
        rows_b = inputs_here[micro_step].reshape(rows_count, width)
        rows_f = rows_b.astype(jnp.float32)
        projected = (
            jnp.einsum("rd,cde->cre", rows_b, wq_all, preferred_element_type=jnp.float32)
            + bias_three
        )
        proj_b = projected.astype(jnp.bfloat16)
        query = proj_b[0].reshape(seqs, local_len, local_heads, HEAD_DIM)
        local_kv = proj_b[1:].reshape(2, seqs, local_len, local_width)
        full_kv = lax.all_gather(local_kv, "ctx", axis=2, tiled=True)
        keys = full_kv[0].reshape(seqs, full_len, local_heads, HEAD_DIM)
        values = full_kv[1].reshape(seqs, full_len, local_heads, HEAD_DIM)
        allowed = ids_here[micro_step][:, None, :, None] == key_ids[micro_step][:, None, None, :]
        probs, log_total = attention_probs(query, keys, allowed, None)
        probs_b = probs.astype(jnp.bfloat16)
        mixed = jnp.einsum("shqk,skhd->sqhd", probs_b, values, preferred_element_type=jnp.float32)
        mixed_b = mixed.reshape(rows_count, local_width).astype(jnp.bfloat16)
        branch = lax.psum(jnp.dot(mixed_b, wo_all, preferred_element_type=jnp.float32), "tp")
        normed1, scale1 = normalize_rows(rows_f + branch + b_out)
        first = normed1 * ln1_gain + ln1_bias
        first_b = first.astype(jnp.bfloat16)
        hidden = jnp.dot(first_b, wu_all, preferred_element_type=jnp.float32) + b_up
        activation, gelu_pull = jax.vjp(
            lambda hidden_in: jax.nn.gelu(hidden_in, approximate=False), hidden
        )
        act_b = activation.astype(jnp.bfloat16)
        second = lax.psum(
            jnp.dot(act_b, wd_all, preferred_element_type=jnp.float32).astype(jnp.bfloat16), "tp"
        ).astype(jnp.float32)
        normed2, scale2 = normalize_rows(first + second + b_down)
        result = normed2 * ln2_gain + ln2_bias
        outputs.append(result.astype(jnp.bfloat16).reshape(seqs, local_len, width))
        incoming = cot_here[micro_step].reshape(rows_count, width).astype(jnp.float32)
        grad_gain2 = grad_gain2 + jnp.sum(incoming * normed2, axis=0)
        grad_shift2 = grad_shift2 + jnp.sum(incoming, axis=0)
        grad_z2 = normalize_back(incoming * ln2_gain, normed2, scale2)
        grad_bdown = grad_bdown + jnp.sum(grad_z2, axis=0)
        grad_second_b = grad_z2.astype(jnp.bfloat16)
        step_wd = jnp.dot(act_b.T, grad_second_b, preferred_element_type=jnp.float32)
        grad_act = jnp.dot(grad_second_b, wd_all.T, preferred_element_type=jnp.float32)
        (grad_hidden,) = gelu_pull(grad_act)
        grad_hidden_b = grad_hidden.astype(jnp.bfloat16)
        grad_bup = grad_bup + jnp.sum(grad_hidden_b.astype(jnp.float32), axis=0)
        step_wu = jnp.dot(first_b.T, grad_hidden_b, preferred_element_type=jnp.float32)
        grad_first = grad_z2 + lax.psum(
            jnp.dot(grad_hidden_b, wu_all.T, preferred_element_type=jnp.float32).astype(
                jnp.bfloat16
            ),
            "tp",
        ).astype(jnp.float32)
        grad_gain1 = grad_gain1 + jnp.sum(grad_first * normed1, axis=0)
        grad_shift1 = grad_shift1 + jnp.sum(grad_first, axis=0)
        grad_z1 = normalize_back(grad_first * ln1_gain, normed1, scale1)
        grad_bout = grad_bout + jnp.sum(grad_z1, axis=0)
        grad_branch_b = grad_z1.astype(jnp.bfloat16)
        step_wo = jnp.dot(mixed_b.T, grad_branch_b, preferred_element_type=jnp.float32)
        grad_mixed_b = jnp.dot(grad_branch_b, wo_all.T, preferred_element_type=jnp.float32).astype(
            jnp.bfloat16
        )
        grad_mixed_b = grad_mixed_b.reshape(seqs, local_len, local_heads, HEAD_DIM)
        recomputed, unused_total = attention_probs(query, keys, allowed, log_total)
        recomputed_b = recomputed.astype(jnp.bfloat16)
        grad_probs = jnp.einsum(
            "sqhd,skhd->shqk", grad_mixed_b, values, preferred_element_type=jnp.float32
        )
        weighted = jnp.sum(recomputed * grad_probs, axis=-1, keepdims=True)
        grad_scores_b = (recomputed * (grad_probs - weighted)).astype(jnp.bfloat16)
        grad_query = (
            jnp.einsum("shqk,skhd->sqhd", grad_scores_b, keys, preferred_element_type=jnp.float32)
            * 0.125
        )
        grad_keys = (
            jnp.einsum("shqk,sqhd->skhd", grad_scores_b, query, preferred_element_type=jnp.float32)
            * 0.125
        )
        grad_values = jnp.einsum(
            "shqk,sqhd->skhd", recomputed_b, grad_mixed_b, preferred_element_type=jnp.float32
        )
        kv_terms = jnp.stack([grad_keys, grad_values]).reshape(2, seqs, full_len, local_width)
        kv_back = lax.psum_scatter(
            kv_terms.astype(jnp.bfloat16), "ctx", scatter_dimension=2, tiled=True
        ).astype(jnp.float32)
        grad_proj_b = jnp.concatenate(
            [
                grad_query.reshape(1, rows_count, local_width).astype(jnp.bfloat16),
                kv_back.reshape(2, rows_count, local_width).astype(jnp.bfloat16),
            ],
            axis=0,
        )
        grad_bqv = grad_bqv + jnp.sum(grad_proj_b[0::2].astype(jnp.float32), axis=1)
        step_wq = jnp.einsum("rd,cre->cde", rows_b, grad_proj_b, preferred_element_type=jnp.float32)
        back_rows = jnp.einsum(
            "cre,cde->rd", grad_proj_b, wq_all, preferred_element_type=jnp.float32
        )
        grad_rows = grad_z1 + lax.psum(back_rows.astype(jnp.bfloat16), "tp").astype(jnp.float32)
        input_grads.append(grad_rows.astype(jnp.bfloat16).reshape(seqs, local_len, width))
        step_grads = (step_wq, step_wo, step_wu, step_wd)
        local_acc = tuple((left + right for left, right in zip(local_acc, step_grads)))
    shard_acc = spread_grads(local_acc)
    small_sums = lax.psum(
        (
            grad_bqv,
            grad_bout,
            grad_gain1,
            grad_shift1,
            grad_bup,
            grad_bdown,
            grad_gain2,
            grad_shift2,
        ),
        "fsdp",
    )
    summed = (
        lax.psum(shard_acc[0].astype(jnp.bfloat16), "ctx").astype(jnp.float32),
        lax.psum(shard_acc[1].astype(jnp.bfloat16), "ctx").astype(jnp.float32),
        lax.psum(shard_acc[2].astype(jnp.bfloat16), "ctx").astype(jnp.float32),
        lax.psum(shard_acc[3].astype(jnp.bfloat16), "ctx").astype(jnp.float32),
        lax.psum(small_sums[0].astype(jnp.bfloat16), "ctx").astype(jnp.float32),
        lax.psum(small_sums[1].astype(jnp.bfloat16), "ctx").astype(jnp.float32),
        lax.psum(small_sums[2].astype(jnp.bfloat16), "ctx").astype(jnp.float32),
        lax.psum(small_sums[3].astype(jnp.bfloat16), "ctx").astype(jnp.float32),
        lax.psum(small_sums[4].astype(jnp.bfloat16), "ctx").astype(jnp.float32),
        lax.psum(small_sums[5].astype(jnp.bfloat16), "ctx").astype(jnp.float32),
        lax.psum(small_sums[6].astype(jnp.bfloat16), "ctx").astype(jnp.float32),
        lax.psum(small_sums[7].astype(jnp.bfloat16), "ctx").astype(jnp.float32),
    )
    stacked_out = jnp.stack(outputs)
    stacked_grad = jnp.stack(input_grads)
    return (
        stacked_out,
        stacked_grad,
        summed[0],
        summed[4],
        summed[1],
        summed[5],
        summed[6],
        summed[7],
        summed[2],
        summed[8],
        summed[3],
        summed[9],
        summed[10],
        summed[11],
    )


def solution(mesh):
    return jax.shard_map(
        body,
        mesh=mesh,
        in_specs=(
            P(None, "fsdp", "ctx", None),
            P(None, "fsdp", "ctx"),
            P(None, "fsdp", "tp"),
            P(None, "tp"),
            P("tp", "fsdp"),
            P(),
            P(),
            P(),
            P("fsdp", "tp"),
            P("tp"),
            P("tp", "fsdp"),
            P(),
            P(),
            P(),
            P(None, "fsdp", "ctx", None),
        ),
        out_specs=(
            P(None, "fsdp", "ctx", None),
            P(None, "fsdp", "ctx", None),
            P(None, "fsdp", "tp"),
            P(None, "tp"),
            P("tp", "fsdp"),
            P(),
            P(),
            P(),
            P("fsdp", "tp"),
            P("tp"),
            P("tp", "fsdp"),
            P(),
            P(),
            P(),
        ),
        check_vma=False,
    )
```

profile of v0, /device:TPU:0, one launch (start us, length us, event | category | flops | bytes accessed | tf_op | source)
XLA Modules:
  0.0 957.4 jit_solution(15539514754937439668)
XLA Ops:
  10.4 42.3 %all-gather.8.cloned.1.call-done = bf16[3,768,384]{2,1,0:T(8,128)(2,1)} async-done(((bf16[3,192,384]{2,1,0:T(8,128)(2,1)}), bf16[3,768,384]{2,1,0:T(8,128)(2,1)}) %all-gather.8.cloned.1.call-update) | async-done | bytes 1769488 | tf_op jit(solution)/shard_map/all_gather | solution.py:25
  52.6 2.2 fusion.45
  55.7 2.2 fusion.44
  58.8 2.2 fusion.42
  61.9 2.3 fusion.43
  65.2 5.2 all_gather.20
  70.3 17.5 %all_gather.42 = bf16[384,768]{0,1:T(8,128)(2,1)} all-gather(bf16[384,192]{0,1:T(8,128)(2,1)S(1)} %copy-done.144), channel_id=1, replica_groups=mesh['fsdp'=4,'ctx'=4,'tp'=2] {'fsdp'}, dimensions={1}, use_global_device_ids=true | all-gather | bytes 737280 | tf_op jit(solution)/shard_map/all_gather | solution.py:26
  98.8 18.0 %all-gather.20.cloned.1.call-done = bf16[2,2,512,384]{3,2,1,0:T(8,128)(2,1)} async-done(((bf16[2,2,128,384]{3,2,1,0:T(8,128)(2,1)}), bf16[2,2,512,384]{3,2,1,0:T(8,128)(2,1)}) %all-gather.20.cloned.1.call-update) | async-done | bytes 1572880 | tf_op jit(solution)/shard_map/all_gather | solution.py:117
  119.5 19.0 %all-gather.18.cloned.1.call-done = bf16[2,2,512,384]{3,2,1,0:T(8,128)(2,1)} async-done(((bf16[2,2,128,384]{3,2,1,0:T(8,128)(2,1)}), bf16[2,2,512,384]{3,2,1,0:T(8,128)(2,1)}) %all-gather.18.cloned.1.call-update) | async-done | bytes 1572880 | tf_op jit(solution)/shard_map/all_gather | solution.py:117
  138.4 2.4 fusion.212
  140.9 2.3 copy.127
  147.9 2.0 fusion.2
  171.0 84.9 %all-reduce.13.cloned.1.call-done = (f32[256,768]{1,0:T(8,128)}, f32[256,768]{1,0:T(8,128)}, f32[256,768]{1,0:T(8,128)}, f32[256,768]{1,0:T(8,128)}) async-done(((f32[256,768]{1,0:T(8,128)}, f32[256,768]{1,0:T(8,128)}, f32[256,768]{1,0:T(8,128)}, f32[256,768]{1,0:T(8,128)}), (f32[256,768]{1,0:T(8,128)}, f32[256,768]{1,0:T(8,128)}, f32[256,768]{1,0:T(8,128)}, ...) | async-done | bytes 3145744 | tf_op jit(solution)/shard_map/psum | solution.py:125
  255.9 2.7 fusion.201
  262.6 45.5 %all-gather.12.cloned.1.call-done = bf16[768,1536]{1,0:T(8,128)(2,1)} async-done(((bf16[192,1536]{1,0:T(8,128)(2,1)}), bf16[768,1536]{1,0:T(8,128)(2,1)}) %all-gather.12.cloned.1.call-update) | async-done | bytes 2359312 | tf_op jit(solution)/shard_map/all_gather | solution.py:27
  308.1 7.9 multiply_convert_fusion.10
  316.1 5.8 multiply_convert_fusion.9
  321.8 37.2 %all-gather.14.cloned.1.call-done = bf16[1536,768]{0,1:T(8,128)(2,1)} async-done(((bf16[1536,192]{0,1:T(8,128)(2,1)}), bf16[1536,768]{0,1:T(8,128)(2,1)}) %all-gather.14.cloned.1.call-update) | async-done | bytes 2359312 | tf_op jit(solution)/shard_map/all_gather | solution.py:28
  359.1 3.6 convolution_convert_fusion.10
  364.8 5.2 multiply_convert_fusion.8
  372.5 5.2 multiply_convert_fusion.11
  380.4 2.5 convert_reduce_fusion.6
  384.0 47.1 %all-reduce.21.cloned.1.call-done = (bf16[256,768]{1,0:T(8,128)(2,1)}, bf16[256,768]{1,0:T(8,128)(2,1)}, bf16[256,768]{1,0:T(8,128)(2,1)}, bf16[256,768]{1,0:T(8,128)(2,1)}) async-done(((bf16[256,768]{1,0:T(8,128)(2,1)}, bf16[256,768]{1,0:T(8,128)(2,1)}, bf16[256,768]{1,0:T(8,128)(2,1)}, bf16[256,768]{1,0:T(8,128)(2,1)}), (bf16[256,768]{1,0:T(8,128)(2,1)}, bf16[256,768]{1,0:T(8,128)(2,1)}, ...) | async-done | bytes 1572880 | tf_op jit(solution)/shard_map/psum | solution.py:134
  433.4 2.0 fusion.196
  436.8 2.6 fusion.64
  439.4 2.2 fusion.71
  461.9 52.0 %all-reduce.19.cloned.1.call-done = (bf16[256,768]{1,0:T(8,128)(2,1)}, bf16[256,768]{1,0:T(8,128)(2,1)}, bf16[256,768]{1,0:T(8,128)(2,1)}, bf16[256,768]{1,0:T(8,128)(2,1)}) async-done(((bf16[256,768]{1,0:T(8,128)(2,1)}, bf16[256,768]{1,0:T(8,128)(2,1)}, bf16[256,768]{1,0:T(8,128)(2,1)}, bf16[256,768]{1,0:T(8,128)(2,1)}), (bf16[256,768]{1,0:T(8,128)(2,1)}, bf16[256,768]{1,0:T(8,128)(2,1)}, ...) | async-done | bytes 1572880 | tf_op jit(solution)/shard_map/psum | solution.py:152
  514.0 3.7 multiply_reduce_fusion.7
  517.9 4.1 fusion.193
  522.0 2.1 fusion.192
  529.5 3.0 convolution_convert_fusion
  538.0 4.9 copy.178
  542.9 4.8 reshape.466
  548.2 2.3 convolution_convert_fusion.18
  554.0 4.1 multiply_reduce_fusion.2
  562.5 5.0 copy.174
  567.5 4.9 reshape.462
  572.5 2.3 convolution_convert_fusion.19
  578.2 3.7 multiply_reduce_fusion.3
  586.3 5.0 copy.172
  591.3 4.8 reshape.460
  597.8 2.4 fusion.194
  605.6 2.6 multiply_reduce_fusion.1
  611.4 2.2 copy.176
  613.6 1.9 reshape.464
  625.6 1.9 fusion.55
  630.6 7.0 reduce-scatter.25.cloned.1.call-done
  638.8 30.0 %reduce-scatter.29.cloned.1.call-done = bf16[128,1536]{1,0:T(8,128)(2,1)} async-done(((bf16[512,1536]{1,0:T(8,128)(2,1)}), bf16[128,1536]{1,0:T(8,128)(2,1)}) %reduce-scatter.29.cloned.1.call-update) | async-done | bytes 393232
  670.0 3.1 fusion.41
  681.0 1.9 fusion.32
  682.9 4.0 copy.180
  689.9 3.2 fusion.183
  697.9 2.2 fusion.180
  701.9 2.4 add_convert_fusion.1
  705.4 2.0 fusion.120
  710.3 2.4 add_convert_fusion
  717.7 19.4 %all-reduce = (bf16[2,384]{1,0:T(2,128)(2,1)S(1)}, bf16[768]{0:T(1024)(128)(2,1)S(1)}, bf16[768]{0:T(1024)(128)(2,1)S(1)}, bf16[768]{0:T(1024)(128)(2,1)S(1)}, b...) all-reduce(f32[2,384]{1,0:T(2,128)S(1)} %add_add_fusion.15, ...), channel_id=1, replica_groups=mesh['fsdp'=4,'ctx'=4,'tp'=2] {'fsdp'}, use_global_device_ids=true, to_apply=%region_70.71 | all-reduce | flops 6912 | bytes 41472 | tf_op jit(solution)/shard_map/psum | solution.py:207
  737.0 11.0 %all-reduce.2 = (bf16[2,384]{1,0:T(2,128)(2,1)S(1)}, bf16[768]{0:T(1024)(128)(2,1)S(1)}, bf16[768]{0:T(1024)(128)(2,1)S(1)}, bf16[768]{0:T(1024)(128)(2,1)S(1)},...) all-reduce(bf16[2,384]{1,0:T(2,128)(2,1)S(1)} %get-tuple-element.10, ...), channel_id=1, replica_groups=mesh['fsdp'=4,'ctx'=4,'tp'=2] {'ctx'}, use_global_device_ids=true, to_apply=%region_71.72 | all-reduce | flops 6912 | bytes 27648 | tf_op jit(solution)/shard_map/psum | solution.py:225
  753.9 16.5 %reduce-scatter.33.cloned.1.call-done = bf16[192,1152]{1,0:T(8,128)(2,1)} async-done(((bf16[768,1152]{1,0:T(8,128)(2,1)}), bf16[192,1152]{1,0:T(8,128)(2,1)}) %reduce-scatter.33.cloned.1.call-update) | async-done | bytes 442384
  773.1 21.2 %reduce-scatter.19.cloned.1.call-done = bf16[384,192]{0,1:T(8,128)(2,1)} async-done(((bf16[384,768]{0,1:T(8,128)(2,1)}), bf16[384,192]{0,1:T(8,128)(2,1)}) %reduce-scatter.19.cloned.1.call-update) | async-done | bytes 147472 | tf_op jit(solution)/shard_map/reduce_scatter | solution.py:37
  794.3 48.7 %reduce-scatter.21.cloned.1.call-done = bf16[192,1536]{1,0:T(8,128)(2,1)} async-done(((bf16[768,1536]{1,0:T(8,128)(2,1)}), bf16[192,1536]{1,0:T(8,128)(2,1)}) %reduce-scatter.21.cloned.1.call-update) | async-done | bytes 589840 | tf_op jit(solution)/shard_map/reduce_scatter | solution.py:40
  843.0 50.0 %reduce-scatter.23.cloned.1.call-done = bf16[1536,192]{0,1:T(8,128)(2,1)} async-done(((bf16[1536,768]{0,1:T(8,128)(2,1)}), bf16[1536,192]{0,1:T(8,128)(2,1)}) %reduce-scatter.23.cloned.1.call-update) | async-done | bytes 589840 | tf_op jit(solution)/shard_map/reduce_scatter | solution.py:43
  895.7 49.2 %all-reduce.15.cloned.1.call-done = (bf16[3,192,384]{1,2,0:T(8,128)(2,1)}, bf16[384,192]{0,1:T(8,128)(2,1)}, bf16[192,1536]{1,0:T(8,128)(2,1)}, bf16[1536,192]{0,1:T(8,128)(2,1)}) async-done(((bf16[3,192,384]{1,2,0:T(8,128)(2,1)}, bf16[384,192]{0,1:T(8,128)(2,1)}, bf16[192,1536]{1,0:T(8,128)(2,1)}, bf16[1536,192]{0,1:T(8,128)(2,1)}), (bf16[3,192,384]{1,2,0:T(8,128)(2,1)}, bf16[384,192]{0,1:T(8,128)(2,1)}, ...) | async-done | bytes 1769488 | tf_op jit(solution)/shard_map/psum | solution.py:221
  944.9 2.3 copy.167
  (731 shorter events, 173.8 us)
Async XLA Ops:
  7.2 45.5 %all-gather.8.cloned.1.call-start = ((), (), s32[]{:S(2)}) async-start(), calls=%async_computation.8 | async-start | bytes 2211840 | tf_op jit(solution)/shard_map/all_gather | solution.py:25
  7.9 85.4 %all-gather.10.cloned.1.call-start = ((), (), s32[]{:S(2)}) async-start(), calls=%async_computation.9 | async-start | bytes 1966080 | tf_op jit(solution)/shard_map/all_gather | solution.py:117
  10.3 44.5 %copy-start.60 = (bf16[1,2,128,768]{3,2,1,0:T(8,128)(2,1)}, bf16[1,2,128,768]{3,2,1,0:T(8,128)(2,1)S(1)}, u32[]{:S(2)}) copy-start(bf16[1,2,128,768]{3,2,1,0:T(8,128)(2,1)S(1)} %get-tuple-element.175) | copy-start | bytes 1179652
  10.3 45.3 %copy-start.58 = (bf16[1,2,128,768]{3,2,1,0:T(8,128)(2,1)}, bf16[1,2,128,768]{3,2,1,0:T(8,128)(2,1)S(1)}, u32[]{:S(2)}) copy-start(bf16[1,2,128,768]{3,2,1,0:T(8,128)(2,1)S(1)} %get-tuple-element.174) | copy-start | bytes 1179652
  10.4 51.5 %copy-start.62 = (bf16[1,2,128,768]{3,2,1,0:T(8,128)(2,1)}, bf16[1,2,128,768]{3,2,1,0:T(8,128)(2,1)S(1)}, u32[]{:S(2)}) copy-start(bf16[1,2,128,768]{3,2,1,0:T(8,128)(2,1)S(1)} %get-tuple-element.177) | copy-start | bytes 1179652
  55.6 40.4 %all-gather.16.cloned.1.call-start = ((), (), s32[]{:S(2)}) async-start(), calls=%async_computation.12 | async-start | bytes 1966080 | tf_op jit(solution)/shard_map/all_gather | solution.py:117
  57.8 31.9 %copy-start.132 = (bf16[3,256,384]{2,1,0:T(8,128)(2,1)}, bf16[3,256,384]{2,1,0:T(8,128)(2,1)S(1)}, u32[]{:S(2)}) copy-start(bf16[3,256,384]{2,1,0:T(8,128)(2,1)S(1)} %fusion.44) | copy-start | bytes 1769476
  58.7 58.0 %all-gather.20.cloned.1.call-start = ((), (), s32[]{:S(2)}) async-start(), calls=%async_computation.14 | async-start | bytes 1966080 | tf_op jit(solution)/shard_map/all_gather | solution.py:117
  60.9 28.8 %copy-start.131 = (bf16[3,256,384]{2,1,0:T(8,128)(2,1)}, bf16[3,256,384]{2,1,0:T(8,128)(2,1)S(1)}, u32[]{:S(2)}) copy-start(bf16[3,256,384]{2,1,0:T(8,128)(2,1)S(1)} %fusion.42) | copy-start | bytes 1769476
  61.8 76.6 %all-gather.18.cloned.1.call-start = ((), (), s32[]{:S(2)}) async-start(), calls=%async_computation.13 | async-start | bytes 1966080 | tf_op jit(solution)/shard_map/all_gather | solution.py:117
  61.9 8.4 copy-start.144
  64.2 25.5 %copy-start.130 = (bf16[3,256,384]{2,1,0:T(8,128)(2,1)}, bf16[3,256,384]{2,1,0:T(8,128)(2,1)S(1)}, u32[]{:S(2)}) copy-start(bf16[3,256,384]{2,1,0:T(8,128)(2,1)S(1)} %fusion.43) | copy-start | bytes 1769476
  65.1 190.8 %all-reduce.13.cloned.1.call-start = ((), (), s32[]{:S(2)}) async-start(), calls=%async_computation.23 | async-start | bytes 6291456 | tf_op jit(solution)/shard_map/psum | solution.py:125
  169.4 86.5 %copy-start.215 = (f32[768]{0:T(1024)S(1)}, f32[768]{0:T(1024)}, u32[]{:S(2)}) copy-start(f32[768]{0:T(1024)} %param.20) | copy-start | bytes 9220
  169.4 138.7 %all-gather.12.cloned.1.call-start = ((), (), s32[]{:S(2)}) async-start(), calls=%async_computation.10 | async-start | bytes 2949120 | tf_op jit(solution)/shard_map/all_gather | solution.py:27
  170.2 188.9 %all-gather.14.cloned.1.call-start = ((), (), s32[]{:S(2)}) async-start(), calls=%async_computation.11 | async-start | bytes 2949120 | tf_op jit(solution)/shard_map/all_gather | solution.py:28
  170.9 260.2 %all-reduce.21.cloned.1.call-start = ((), (), s32[]{:S(2)}) async-start(), calls=%async_computation.27 | async-start | bytes 3145728 | tf_op jit(solution)/shard_map/psum | solution.py:134
  258.7 49.4 %copy-start.119 = (f32[768]{0:T(1024)S(1)}, f32[768]{0:T(1024)}, u32[]{:S(2)}) copy-start(f32[768]{0:T(1024)} %param.21) | copy-start | bytes 9220
  258.7 49.4 %copy-start.120 = (f32[768]{0:T(1024)S(1)}, f32[768]{0:T(1024)}, u32[]{:S(2)}) copy-start(f32[768]{0:T(1024)} %param.22) | copy-start | bytes 9220
  308.1 8.0 copy-start.19
  308.1 8.0 copy-start.158
  308.1 7.9 copy-start.174
  308.1 7.9 copy-start.220
  308.1 7.9 copy-start.226
  380.2 133.7 %all-reduce.19.cloned.1.call-start = ((), (), s32[]{:S(2)}) async-start(), calls=%async_computation.26 | async-start | bytes 3145728 | tf_op jit(solution)/shard_map/psum | solution.py:152
  441.6 15.1 %copy-start.50 = (f32[256,768]{1,0:T(8,128)}, f32[256,768]{1,0:T(8,128)S(1)}, u32[]{:S(2)}) copy-start(f32[256,768]{1,0:T(8,128)S(1)} %get-tuple-element.171) | copy-start | bytes 2359300
  442.5 4.5 copy-start.36
  442.5 6.1 copy-start.53
  442.5 10.1 %copy-start.42 = (f32[256,768]{1,0:T(8,128)}, f32[256,768]{1,0:T(8,128)S(1)}, u32[]{:S(2)}) copy-start(f32[256,768]{1,0:T(8,128)S(1)} %get-tuple-element.168) | copy-start | bytes 2359300
  461.6 166.4 %reduce-scatter.31.cloned.1.call-start = ((), (), s32[]{:S(2)}) async-start(), calls=%async_computation.21 | async-start | bytes 1966080
  513.9 3.8 copy-start.155
  513.9 3.8 copy-start.160
  517.8 4.2 copy-start.16
  517.8 4.2 copy-start.43
  517.8 4.1 copy-start.113
  517.8 4.1 copy-start.114
  517.8 4.1 copy-start.164
  517.8 4.1 copy-start.179
  547.8 81.5 %reduce-scatter.27.cloned.1.call-start = ((), (), s32[]{:S(2)}) async-start(), calls=%async_computation.19 | async-start | bytes 1966080
  554.0 4.1 copy-start.3
  554.0 4.1 copy-start.77
  554.0 4.1 copy-start.148
  572.4 65.2 %reduce-scatter.25.cloned.1.call-start = ((), (), s32[]{:S(2)}) async-start(), calls=%async_computation.18 | async-start | bytes 1966080
  596.2 72.6 %reduce-scatter.29.cloned.1.call-start = ((), (), s32[]{:S(2)}) async-start(), calls=%async_computation.20 | async-start | bytes 1966080
  596.4 4.7 copy-start.8
  615.6 4.5 copy-start.30
  615.6 137.2 %all-reduce.17.cloned.1.call-start = ((), (), s32[]{:S(2)}) async-start(), calls=%async_computation.25 | async-start | bytes 3145728 | tf_op jit(solution)/shard_map/psum | solution.py:202
  625.6 49.0 %copy-start.98 = (bf16[1,256,384]{2,1,0:T(8,128)(2,1)}, bf16[1,256,384]{2,1,0:T(8,128)(2,1)S(1)}, u32[]{:S(2)}) copy-start(bf16[1,256,384]{2,1,0:T(8,128)(2,1)S(1)} %copy.141) | copy-start | bytes 589828
  628.1 49.8 %copy-start.101 = (bf16[1,256,384]{2,1,0:T(8,128)(2,1)}, bf16[1,256,384]{2,1,0:T(8,128)(2,1)S(1)}, u32[]{:S(2)}) copy-start(bf16[1,256,384]{2,1,0:T(8,128)(2,1)S(1)} %copy.155) | copy-start | bytes 589828
  629.3 51.7 %copy-start.64 = (bf16[2,2,128,384]{3,2,1,0:T(8,128)(2,1)}, bf16[2,2,128,384]{3,2,1,0:T(8,128)(2,1)S(1)}, u32[]{:S(2)}) copy-start(bf16[2,2,128,384]{3,2,1,0:T(8,128)(2,1)S(1)} %copy.161) | copy-start | bytes 1179652
  630.6 49.4 %copy-start.66 = (bf16[2,2,128,384]{3,2,1,0:T(8,128)(2,1)}, bf16[2,2,128,384]{3,2,1,0:T(8,128)(2,1)S(1)}, u32[]{:S(2)}) copy-start(bf16[2,2,128,384]{3,2,1,0:T(8,128)(2,1)S(1)} %copy.147) | copy-start | bytes 1179652
  630.6 39.3 %copy-start.111 = (bf16[1,256,384]{2,1,0:T(8,128)(2,1)S(1)}, bf16[1,256,384]{2,1,0:T(8,128)(2,1)}, u32[]{:S(2)}) copy-start(bf16[1,256,384]{2,1,0:T(8,128)(2,1)} %copy.162) | copy-start | bytes 589828
  638.8 40.5 %copy-start.68 = (bf16[2,2,128,384]{3,2,1,0:T(8,128)(2,1)}, bf16[2,2,128,384]{3,2,1,0:T(8,128)(2,1)S(1)}, u32[]{:S(2)}) copy-start(bf16[2,2,128,384]{3,2,1,0:T(8,128)(2,1)S(1)} %copy.140) | copy-start | bytes 1179652
  669.9 7.9 copy-start.70
  677.6 92.8 %reduce-scatter.33.cloned.1.call-start = ((), (), s32[]{:S(2)}) async-start(), calls=%async_computation.22 | async-start | bytes 2211840
  688.5 4.5 copy-start.48
  688.5 4.5 copy-start.108
  688.5 105.8 %reduce-scatter.19.cloned.1.call-start = ((), (), s32[]{:S(2)}) async-start(), calls=%async_computation.15 | async-start | bytes 737280 | tf_op jit(solution)/shard_map/reduce_scatter | solution.py:37
  697.8 145.2 %reduce-scatter.21.cloned.1.call-start = ((), (), s32[]{:S(2)}) async-start(), calls=%async_computation.16 | async-start | bytes 2949120 | tf_op jit(solution)/shard_map/reduce_scatter | solution.py:40
  704.3 188.6 %reduce-scatter.23.cloned.1.call-start = ((), (), s32[]{:S(2)}) async-start(), calls=%async_computation.17 | async-start | bytes 2949120 | tf_op jit(solution)/shard_map/reduce_scatter | solution.py:43
  712.9 232.0 %all-reduce.15.cloned.1.call-start = ((), (), s32[]{:S(2)}) async-start(), calls=%async_computation.24 | async-start | bytes 3833856 | tf_op jit(solution)/shard_map/psum | solution.py:221
  717.2 35.6 %copy-start.49 = (f32[256,768]{1,0:T(8,128)S(1)}, f32[256,768]{1,0:T(8,128)}, u32[]{:S(2)}) copy-start(f32[256,768]{1,0:T(8,128)} %get-tuple-element.139) | copy-start | bytes 2359300
  771.8 121.2 %copy-start.142 = (bf16[256,768]{1,0:T(8,128)(2,1)S(1)}, bf16[256,768]{1,0:T(8,128)(2,1)}, u32[]{:S(2)}) copy-start(bf16[256,768]{1,0:T(8,128)(2,1)} %get-tuple-element.126) | copy-start | bytes 1179652
  944.9 4.2 copy-start.137
  (197 other events, 371.4 us)
Sparse Core Ops, SparseCore 0:
  9.6 43.0 all-gather.7
  55.7 18.6 all-gather.9
  76.0 19.6 all-gather.15
  97.1 19.6 all-gather.19
  118.7 19.6 all-gather.17
  169.6 86.3 all-reduce.12
  257.6 50.4 all-gather.11
  309.7 49.2 all-gather.13
  380.3 50.8 all-reduce.20
  461.8 52.0 all-reduce.18
  547.9 28.1 reduce-scatter.30
  578.5 28.1 reduce-scatter.26
  609.4 28.1 reduce-scatter.24
  640.6 28.1 reduce-scatter.28
  677.7 52.0 all-reduce.16
  732.0 38.3 reduce-scatter.32
  773.2 21.0 reduce-scatter.18
  796.6 46.3 reduce-scatter.20
  845.4 47.5 reduce-scatter.22
  896.2 48.6 all-reduce.14
where the time goes:
time: 963 us; the launch traced here: 957 us
  waiting for transfers between devices  571 us (59%)
  matrix products  130 us (13%)
  local copies, waits for them, and re-layouts  124 us (13%)
  other arithmetic  59.6 us (6%)
  blocking collectives  53.1 us (6%)
  between operations  17.5 us (2%)
    psum x1, waiting for transfers between devices, body(): lax.psum(jnp.dot(mixed_b, wo_all, preferred_element_type=jnp.float32), 'tp')  84.9 us
    unnamed x493, local copies, waits for them, and re-layouts  79.3 us
    unnamed x25, waiting for transfers between devices  55.9 us
    psum x1, waiting for transfers between devices, body(): lax.psum(jnp.dot(grad_hidden_b, wu_all.T, preferred_element_type=jnp.floa...  52 us
    reduce_scatter x1, waiting for transfers between devices, spread_grads(): lax.psum_scatter(grads[3].astype(jnp.bfloat16), 'fsdp', scatter_dimension...  50 us
    psum x1, waiting for transfers between devices, body(): lax.psum(shard_acc[0].astype(jnp.bfloat16), 'ctx').astype(jnp.float32)  49.2 us
    reduce_scatter x1, waiting for transfers between devices, spread_grads(): lax.psum_scatter(grads[2].astype(jnp.bfloat16), 'fsdp', scatter_dimension...  48.7 us
    psum x1, waiting for transfers between devices, body(): lax.psum(jnp.dot(act_b, wd_all, preferred_element_type=jnp.float32).astyp...  47.1 us
  transfers between devices with their start and end apart: 20, of which 15 were waited for; matrix products, arithmetic and copies ran while one was open for 17% of the time, Pallas kernels for 0%

commit v1 on v0

--- a/solution.py
+++ b/solution.py
@@ -4,6 +4,23 @@
 from jax.sharding import PartitionSpec as P
 
 HEAD_DIM = 64
+
+
+def in_order(pieces, dim):
+    shape = list(pieces.shape[1:])
+    shape[dim] *= pieces.shape[0]
+    return jnp.moveaxis(pieces, 0, dim).reshape(shape)
+
+
+def ring_gather(x, axis, dim):
+    size = lax.axis_size(axis)
+    upward = [(i, (i + 1) % size) for i in range(size)]
+    blocks = [x]
+    while len(blocks) < size:
+        blocks.append(lax.ppermute(blocks[-1], axis, upward))
+    index = lax.axis_index(axis)
+    blocks = jnp.stack(blocks)[(index - jnp.arange(size)) % size]
+    return in_order(blocks, dim)
 
 
 def normalize_rows(values_in):
@@ -24,7 +41,7 @@
     return (
         lax.all_gather(weights[0], "fsdp", axis=1, tiled=True),
         lax.all_gather(weights[1], "fsdp", axis=1, tiled=True),
-        lax.all_gather(weights[2], "fsdp", axis=0, tiled=True),
+        ring_gather(weights[2], "fsdp", 0),
         lax.all_gather(weights[3], "fsdp", axis=1, tiled=True),
     )
 

time: 963 us -> 899 us (0.934)
  waiting for transfers between devices: 571 us -> 503 us
    psum x1, waiting for transfers between devices: 84.9 us -> 28.3 us  [body(): lax.psum(jnp.dot(mixed_b, wo_all, preferred_element_type=jnp.float32), 'tp')]
    ppermute x0 -> x3, waiting for transfers between devices: none -> 48.3 us  [ring_gather(): blocks.append(lax.ppermute(blocks[-1], axis, upward))]
    all_gather x1 -> x0, waiting for transfers between devices: 45.5 us -> none  [collect_weights(): lax.all_gather(weights[2], 'fsdp', axis=0, tiled=True)]
    all_gather x1, waiting for transfers between devices: 37.2 us -> 24.6 us  [collect_weights(): lax.all_gather(weights[3], 'fsdp', axis=1, tiled=True)]
    unnamed x25 -> x24, waiting for transfers between devices: 55.9 us -> 54.7 us
    unnamed x493 -> x481, local copies, waits for them, and re-layouts: 79.3 us -> 78.9 us
  transfers between devices with their start and end apart: 20 -> 22, of which waited for: 15 -> 17; matrix products, arithmetic and copies ran while one was open for 17% -> 20% of each run, Pallas kernels for 0% -> 0%
where the time goes in v1:
time: 899 us; the launch traced here: 894 us
  waiting for transfers between devices  503 us (56%)
  matrix products  128 us (14%)
  local copies, waits for them, and re-layouts  127 us (14%)
  other arithmetic  61.1 us (7%)
  blocking collectives  53.1 us (6%)
  between operations  17.2 us (2%)
    unnamed x481, local copies, waits for them, and re-layouts  78.9 us
    unnamed x24, waiting for transfers between devices  54.7 us
    psum x1, waiting for transfers between devices, body(): lax.psum(jnp.dot(grad_hidden_b, wu_all.T, preferred_element_type=jnp.floa...  51.9 us
    reduce_scatter x1, waiting for transfers between devices, spread_grads(): lax.psum_scatter(grads[3].astype(jnp.bfloat16), 'fsdp', scatter_dimension...  49.8 us
    psum x1, waiting for transfers between devices, body(): lax.psum(shard_acc[0].astype(jnp.bfloat16), 'ctx').astype(jnp.float32)  49.3 us
    reduce_scatter x1, waiting for transfers between devices, spread_grads(): lax.psum_scatter(grads[2].astype(jnp.bfloat16), 'fsdp', scatter_dimension...  48.7 us
    ppermute x3, waiting for transfers between devices, ring_gather(): blocks.append(lax.ppermute(blocks[-1], axis, upward))  48.3 us
    psum x1, waiting for transfers between devices, body(): lax.psum(jnp.dot(act_b, wd_all, preferred_element_type=jnp.float32).astyp...  47.2 us
  transfers between devices with their start and end apart: 22, of which 17 were waited for; matrix products, arithmetic and copies ran while one was open for 20% of the time, Pallas kernels for 0%

profile of v1, /device:TPU:0, one launch (start us, length us, event | category | flops | bytes accessed | tf_op | source)
XLA Modules:
  0.0 893.6 jit_solution(1812425311172981996)
XLA Ops:
  10.4 42.3 %all-gather.7.cloned.1.call-done = bf16[3,768,384]{2,1,0:T(8,128)(2,1)} async-done(((bf16[3,192,384]{2,1,0:T(8,128)(2,1)}), bf16[3,768,384]{2,1,0:T(8,128)(2,1)}) %all-gather.7.cloned.1.call-update) | async-done | bytes 1769488 | tf_op jit(solution)/shard_map/all_gather | solution.py:42
  52.6 2.2 fusion.45
  55.7 2.2 fusion.44
  58.8 2.2 fusion.42
  62.0 2.3 fusion.43
  65.2 5.2 all_gather.35
  70.4 17.5 %all_gather.36 = bf16[384,768]{0,1:T(8,128)(2,1)} all-gather(bf16[384,192]{0,1:T(8,128)(2,1)S(1)} %copy-done.144), channel_id=1, replica_groups=mesh['fsdp'=4,'ctx'=4,'tp'=2] {'fsdp'}, dimensions={1}, use_global_device_ids=true | all-gather | bytes 737280 | tf_op jit(solution)/shard_map/all_gather | solution.py:43
  98.8 17.9 %all-gather.17.cloned.1.call-done = bf16[2,2,512,384]{3,2,1,0:T(8,128)(2,1)} async-done(((bf16[2,2,128,384]{3,2,1,0:T(8,128)(2,1)}), bf16[2,2,512,384]{3,2,1,0:T(8,128)(2,1)}) %all-gather.17.cloned.1.call-update) | async-done | bytes 1572880 | tf_op jit(solution)/shard_map/all_gather | solution.py:134
  119.5 18.9 %all-gather.15.cloned.1.call-done = bf16[2,2,512,384]{3,2,1,0:T(8,128)(2,1)} async-done(((bf16[2,2,128,384]{3,2,1,0:T(8,128)(2,1)}), bf16[2,2,512,384]{3,2,1,0:T(8,128)(2,1)}) %all-gather.15.cloned.1.call-update) | async-done | bytes 1572880 | tf_op jit(solution)/shard_map/all_gather | solution.py:134
  138.4 2.4 fusion.214
  140.9 2.3 copy.127
  147.9 2.0 fusion.2
  171.1 16.0 %collective-permute-done = bf16[192,1536]{1,0:T(8,128)(2,1)S(1)} collective-permute-done((bf16[192,1536]{1,0:T(8,128)(2,1)}, bf16[192,1536]{1,0:T(8,128)(2,1)S(1)}, u32[]{:S(2)}, u32[]{:S(2)}) %collective-permute-start) | collective-permute-done | bytes 589856 | tf_op jit(solution)/shard_map/ppermute | solution.py:20
  187.9 16.5 %collective-permute-done.1 = bf16[192,1536]{1,0:T(8,128)(2,1)} collective-permute-done((bf16[192,1536]{1,0:T(8,128)(2,1)S(1)}, bf16[192,1536]{1,0:T(8,128)(2,1)}, u32[]{:S(2)}, u32[]{:S(2)}) %collective-permute-start.1) | collective-permute-done | bytes 589856 | tf_op jit(solution)/shard_map/ppermute | solution.py:20
  204.6 15.7 %collective-permute-done.2 = bf16[192,1536]{1,0:T(8,128)(2,1)} collective-permute-done((bf16[192,1536]{1,0:T(8,128)(2,1)}, bf16[192,1536]{1,0:T(8,128)(2,1)}, u32[]{:S(2)}, u32[]{:S(2)}) %collective-permute-start.2) | collective-permute-done | bytes 589856 | tf_op jit(solution)/shard_map/ppermute | solution.py:20
  220.3 3.7 pad_maximum_fusion
  224.0 3.8 gather_fusion
  227.7 28.3 %all-reduce.13.cloned.1.call-done = (f32[256,768]{1,0:T(8,128)}, f32[256,768]{1,0:T(8,128)}, f32[256,768]{1,0:T(8,128)}, f32[256,768]{1,0:T(8,128)}) async-done(((f32[256,768]{1,0:T(8,128)}, f32[256,768]{1,0:T(8,128)}, f32[256,768]{1,0:T(8,128)}, f32[256,768]{1,0:T(8,128)}), (f32[256,768]{1,0:T(8,128)}, f32[256,768]{1,0:T(8,128)}, f32[256,768]{1,0:T(8,128)}, ...) | async-done | bytes 3145744 | tf_op jit(solution)/shard_map/psum | solution.py:142
  256.0 2.7 fusion.203
  261.5 5.8 multiply_convert_fusion.10
  267.4 5.4 multiply_convert_fusion.9
  272.8 5.4 multiply_convert_fusion.8
  278.2 5.4 multiply_convert_fusion.11
  283.6 24.6 %all-gather.11.cloned.1.call-done = bf16[1536,768]{0,1:T(8,128)(2,1)} async-done(((bf16[1536,192]{0,1:T(8,128)(2,1)}), bf16[1536,768]{0,1:T(8,128)(2,1)}) %all-gather.11.cloned.1.call-update) | async-done | bytes 2359312 | tf_op jit(solution)/shard_map/all_gather | solution.py:45
  308.2 3.6 convolution_convert_fusion.10
  316.7 2.5 convert_reduce_fusion.6
  320.4 47.2 %all-reduce.21.cloned.1.call-done = (bf16[256,768]{1,0:T(8,128)(2,1)}, bf16[256,768]{1,0:T(8,128)(2,1)}, bf16[256,768]{1,0:T(8,128)(2,1)}, bf16[256,768]{1,0:T(8,128)(2,1)}) async-done(((bf16[256,768]{1,0:T(8,128)(2,1)}, bf16[256,768]{1,0:T(8,128)(2,1)}, bf16[256,768]{1,0:T(8,128)(2,1)}, bf16[256,768]{1,0:T(8,128)(2,1)}), (bf16[256,768]{1,0:T(8,128)(2,1)}, bf16[256,768]{1,0:T(8,128)(2,1)}, ...) | async-done | bytes 1572880 | tf_op jit(solution)/shard_map/psum | solution.py:151
  373.1 2.6 fusion.64
  375.8 2.2 fusion.71
  398.4 51.9 %all-reduce.19.cloned.1.call-done = (bf16[256,768]{1,0:T(8,128)(2,1)}, bf16[256,768]{1,0:T(8,128)(2,1)}, bf16[256,768]{1,0:T(8,128)(2,1)}, bf16[256,768]{1,0:T(8,128)(2,1)}) async-done(((bf16[256,768]{1,0:T(8,128)(2,1)}, bf16[256,768]{1,0:T(8,128)(2,1)}, bf16[256,768]{1,0:T(8,128)(2,1)}, bf16[256,768]{1,0:T(8,128)(2,1)}), (bf16[256,768]{1,0:T(8,128)(2,1)}, bf16[256,768]{1,0:T(8,128)(2,1)}, ...) | async-done | bytes 1572880 | tf_op jit(solution)/shard_map/psum | solution.py:169
  450.4 3.7 multiply_reduce_fusion.7
  454.3 4.1 fusion.195
  458.4 2.1 fusion.194
  465.8 3.0 convolution_convert_fusion
  474.3 4.9 copy.178
  479.3 4.8 reshape.530
  484.6 2.3 convolution_convert_fusion.18
  490.3 4.1 multiply_reduce_fusion.2
  498.8 5.0 copy.174
  503.8 4.9 reshape.526
  508.8 2.3 convolution_convert_fusion.19
  514.6 3.7 multiply_reduce_fusion.3
  522.6 5.0 copy.172
  527.7 4.8 reshape.524
  534.2 2.4 fusion.196
  542.0 2.6 multiply_reduce_fusion.1
  547.8 2.2 copy.176
  567.0 7.0 reduce-scatter.25.cloned.1.call-done
  575.2 30.2 %reduce-scatter.29.cloned.1.call-done = bf16[128,1536]{1,0:T(8,128)(2,1)} async-done(((bf16[512,1536]{1,0:T(8,128)(2,1)}), bf16[128,1536]{1,0:T(8,128)(2,1)}) %reduce-scatter.29.cloned.1.call-update) | async-done | bytes 393232
  606.5 3.1 fusion.41
  619.5 4.0 copy.180
  626.4 3.1 fusion.185
  634.5 2.2 fusion.182
  638.4 2.4 add_convert_fusion.1
  642.0 2.0 fusion.120
  646.9 2.4 add_convert_fusion
  654.2 19.4 %all-reduce = (bf16[2,384]{1,0:T(2,128)(2,1)S(1)}, bf16[768]{0:T(1024)(128)(2,1)S(1)}, bf16[768]{0:T(1024)(128)(2,1)S(1)}, bf16[768]{0:T(1024)(128)(2,1)S(1)}, b...) all-reduce(f32[2,384]{1,0:T(2,128)S(1)} %add_add_fusion.15, ...), channel_id=1, replica_groups=mesh['fsdp'=4,'ctx'=4,'tp'=2] {'fsdp'}, use_global_device_ids=true, to_apply=%region_70.71 | all-reduce | flops 6912 | bytes 41472 | tf_op jit(solution)/shard_map/psum | solution.py:224
  673.5 11.0 %all-reduce.2 = (bf16[2,384]{1,0:T(2,128)(2,1)S(1)}, bf16[768]{0:T(1024)(128)(2,1)S(1)}, bf16[768]{0:T(1024)(128)(2,1)S(1)}, bf16[768]{0:T(1024)(128)(2,1)S(1)},...) all-reduce(bf16[2,384]{1,0:T(2,128)(2,1)S(1)} %get-tuple-element.10, ...), channel_id=1, replica_groups=mesh['fsdp'=4,'ctx'=4,'tp'=2] {'ctx'}, use_global_device_ids=true, to_apply=%region_71.72 | all-reduce | flops 6912 | bytes 27648 | tf_op jit(solution)/shard_map/psum | solution.py:242
  690.4 16.5 %reduce-scatter.33.cloned.1.call-done = bf16[192,1152]{1,0:T(8,128)(2,1)} async-done(((bf16[768,1152]{1,0:T(8,128)(2,1)}), bf16[192,1152]{1,0:T(8,128)(2,1)}) %reduce-scatter.33.cloned.1.call-update) | async-done | bytes 442384
  709.6 21.2 %reduce-scatter.19.cloned.1.call-done = bf16[384,192]{0,1:T(8,128)(2,1)} async-done(((bf16[384,768]{0,1:T(8,128)(2,1)}), bf16[384,192]{0,1:T(8,128)(2,1)}) %reduce-scatter.19.cloned.1.call-update) | async-done | bytes 147472 | tf_op jit(solution)/shard_map/reduce_scatter | solution.py:54
  730.9 48.7 %reduce-scatter.21.cloned.1.call-done = bf16[192,1536]{1,0:T(8,128)(2,1)} async-done(((bf16[768,1536]{1,0:T(8,128)(2,1)}), bf16[192,1536]{1,0:T(8,128)(2,1)}) %reduce-scatter.21.cloned.1.call-update) | async-done | bytes 589840 | tf_op jit(solution)/shard_map/reduce_scatter | solution.py:57
  779.5 49.8 %reduce-scatter.23.cloned.1.call-done = bf16[1536,192]{0,1:T(8,128)(2,1)} async-done(((bf16[1536,768]{0,1:T(8,128)(2,1)}), bf16[1536,192]{0,1:T(8,128)(2,1)}) %reduce-scatter.23.cloned.1.call-update) | async-done | bytes 589840 | tf_op jit(solution)/shard_map/reduce_scatter | solution.py:60
  832.1 49.3 %all-reduce.15.cloned.1.call-done = (bf16[3,192,384]{1,2,0:T(8,128)(2,1)}, bf16[384,192]{0,1:T(8,128)(2,1)}, bf16[192,1536]{1,0:T(8,128)(2,1)}, bf16[1536,192]{0,1:T(8,128)(2,1)}) async-done(((bf16[3,192,384]{1,2,0:T(8,128)(2,1)}, bf16[384,192]{0,1:T(8,128)(2,1)}, bf16[192,1536]{1,0:T(8,128)(2,1)}, bf16[1536,192]{0,1:T(8,128)(2,1)}), (bf16[3,192,384]{1,2,0:T(8,128)(2,1)}, bf16[384,192]{0,1:T(8,128)(2,1)}, ...) | async-done | bytes 1769488 | tf_op jit(solution)/shard_map/psum | solution.py:238
  881.5 2.3 copy.167
  (726 shorter events, 179.1 us)
Async XLA Ops:
  7.2 45.5 %all-gather.7.cloned.1.call-start = ((), (), s32[]{:S(2)}) async-start(), calls=%async_computation.8 | async-start | bytes 2211840 | tf_op jit(solution)/shard_map/all_gather | solution.py:42
  7.9 85.4 %all-gather.9.cloned.1.call-start = ((), (), s32[]{:S(2)}) async-start(), calls=%async_computation.9 | async-start | bytes 1966080 | tf_op jit(solution)/shard_map/all_gather | solution.py:134
  10.3 44.5 %copy-start.57 = (bf16[1,2,128,768]{3,2,1,0:T(8,128)(2,1)}, bf16[1,2,128,768]{3,2,1,0:T(8,128)(2,1)S(1)}, u32[]{:S(2)}) copy-start(bf16[1,2,128,768]{3,2,1,0:T(8,128)(2,1)S(1)} %get-tuple-element.175) | copy-start | bytes 1179652
  10.3 45.3 %copy-start.55 = (bf16[1,2,128,768]{3,2,1,0:T(8,128)(2,1)}, bf16[1,2,128,768]{3,2,1,0:T(8,128)(2,1)S(1)}, u32[]{:S(2)}) copy-start(bf16[1,2,128,768]{3,2,1,0:T(8,128)(2,1)S(1)} %get-tuple-element.174) | copy-start | bytes 1179652
  10.4 51.6 %copy-start.59 = (bf16[1,2,128,768]{3,2,1,0:T(8,128)(2,1)}, bf16[1,2,128,768]{3,2,1,0:T(8,128)(2,1)S(1)}, u32[]{:S(2)}) copy-start(bf16[1,2,128,768]{3,2,1,0:T(8,128)(2,1)S(1)} %get-tuple-element.177) | copy-start | bytes 1179652
  55.6 40.5 %all-gather.13.cloned.1.call-start = ((), (), s32[]{:S(2)}) async-start(), calls=%async_computation.11 | async-start | bytes 1966080 | tf_op jit(solution)/shard_map/all_gather | solution.py:134
  57.8 31.9 %copy-start.131 = (bf16[3,256,384]{2,1,0:T(8,128)(2,1)}, bf16[3,256,384]{2,1,0:T(8,128)(2,1)S(1)}, u32[]{:S(2)}) copy-start(bf16[3,256,384]{2,1,0:T(8,128)(2,1)S(1)} %fusion.44) | copy-start | bytes 1769476
  58.7 58.0 %all-gather.17.cloned.1.call-start = ((), (), s32[]{:S(2)}) async-start(), calls=%async_computation.13 | async-start | bytes 1966080 | tf_op jit(solution)/shard_map/all_gather | solution.py:134
  61.0 28.8 %copy-start.130 = (bf16[3,256,384]{2,1,0:T(8,128)(2,1)}, bf16[3,256,384]{2,1,0:T(8,128)(2,1)S(1)}, u32[]{:S(2)}) copy-start(bf16[3,256,384]{2,1,0:T(8,128)(2,1)S(1)} %fusion.42) | copy-start | bytes 1769476
  61.9 76.6 %all-gather.15.cloned.1.call-start = ((), (), s32[]{:S(2)}) async-start(), calls=%async_computation.12 | async-start | bytes 1966080 | tf_op jit(solution)/shard_map/all_gather | solution.py:134
  61.9 8.4 copy-start.144
  64.2 25.6 %copy-start.129 = (bf16[3,256,384]{2,1,0:T(8,128)(2,1)}, bf16[3,256,384]{2,1,0:T(8,128)(2,1)S(1)}, u32[]{:S(2)}) copy-start(bf16[3,256,384]{2,1,0:T(8,128)(2,1)S(1)} %fusion.43) | copy-start | bytes 1769476
  65.1 190.9 %all-reduce.13.cloned.1.call-start = ((), (), s32[]{:S(2)}) async-start(), calls=%async_computation.22 | async-start | bytes 6291456 | tf_op jit(solution)/shard_map/psum | solution.py:142
  169.5 138.7 %all-gather.11.cloned.1.call-start = ((), (), s32[]{:S(2)}) async-start(), calls=%async_computation.10 | async-start | bytes 2949120 | tf_op jit(solution)/shard_map/all_gather | solution.py:45
  169.6 17.5 %collective-permute-start = (bf16[192,1536]{1,0:T(8,128)(2,1)}, bf16[192,1536]{1,0:T(8,128)(2,1)S(1)}, u32[]{:S(2)}, u32[]{:S(2)}) collective-permute-start(bf16[192,1536]{1,0:T(8,128)(2,1)} %param.23), channel_id=1, source_target_pairs={{0,8},{8,16},{16,24},{24,0},{1,9},{9,17},{17,25},{25,1},{2,10},{10... | collective-permute-start | bytes 1769480 | tf_op jit(solution)/shard_map/ppermute | solution.py:20
  187.9 16.5 %collective-permute-start.1 = (bf16[192,1536]{1,0:T(8,128)(2,1)S(1)}, bf16[192,1536]{1,0:T(8,128)(2,1)}, u32[]{:S(2)}, u32[]{:S(2)}) collective-permute-start(bf16[192,1536]{1,0:T(8,128)(2,1)S(1)} %collective-permute-done), channel_id=1, source_target_pairs={{0,8},{8,16},{16,24},{24,0},{1,9},{9,17},{17,25},{25,1},{2,10},{10... | collective-permute-start | bytes 1769480 | tf_op jit(solution)/shard_map/ppermute | solution.py:20
  204.5 15.8 %collective-permute-start.2 = (bf16[192,1536]{1,0:T(8,128)(2,1)}, bf16[192,1536]{1,0:T(8,128)(2,1)}, u32[]{:S(2)}, u32[]{:S(2)}) collective-permute-start(bf16[192,1536]{1,0:T(8,128)(2,1)} %collective-permute-done.1), channel_id=1, source_target_pairs={{0,8},{8,16},{16,24},{24,0},{1,9},{9,17},{17,25},{25,1},{2,10},{10... | collective-permute-start | bytes 1769480 | tf_op jit(solution)/shard_map/ppermute | solution.py:20
  204.5 163.1 %all-reduce.21.cloned.1.call-start = ((), (), s32[]{:S(2)}) async-start(), calls=%async_computation.26 | async-start | bytes 3145728 | tf_op jit(solution)/shard_map/psum | solution.py:151
  224.0 32.1 %copy-start.213 = (f32[768]{0:T(1024)S(1)}, f32[768]{0:T(1024)}, u32[]{:S(2)}) copy-start(f32[768]{0:T(1024)} %param.20) | copy-start | bytes 9220
  258.7 8.7 copy-start.17
  258.7 14.0 %copy-start.21 = (f32[256,768]{1,0:T(8,128)}, f32[256,768]{1,0:T(8,128)S(1)}, u32[]{:S(2)}) copy-start(f32[256,768]{1,0:T(8,128)S(1)} %get-tuple-element.216) | copy-start | bytes 2359300
  258.7 19.5 %copy-start.9 = (f32[256,768]{1,0:T(8,128)}, f32[256,768]{1,0:T(8,128)S(1)}, u32[]{:S(2)}) copy-start(f32[256,768]{1,0:T(8,128)S(1)} %get-tuple-element.218) | copy-start | bytes 2359300
  258.8 8.6 copy-start.156
  258.8 14.0 %copy-start.164 = (f32[256]{0:T(256)}, f32[256]{0:T(256)S(1)}, u32[]{:S(2)}) copy-start(f32[256]{0:T(256)S(1)} %broadcast_multiply_fusion.13) | copy-start | bytes 3076
  258.8 19.4 %copy-start.152 = (f32[256]{0:T(256)}, f32[256]{0:T(256)S(1)}, u32[]{:S(2)}) copy-start(f32[256]{0:T(256)S(1)} %broadcast_multiply_fusion.19) | copy-start | bytes 3076
  259.1 19.1 %copy-start.167 = (f32[256]{0:T(256)}, f32[256]{0:T(256)S(1)}, u32[]{:S(2)}) copy-start(f32[256]{0:T(256)S(1)} %add_rsqrt_fusion.7) | copy-start | bytes 3076
  259.3 13.4 %copy-start.179 = (f32[256]{0:T(256)}, f32[256]{0:T(256)S(1)}, u32[]{:S(2)}) copy-start(f32[256]{0:T(256)S(1)} %add_rsqrt_fusion.1) | copy-start | bytes 3076
  259.6 7.8 copy-start.171
  259.8 7.5 copy-start.175
  316.5 133.8 %all-reduce.19.cloned.1.call-start = ((), (), s32[]{:S(2)}) async-start(), calls=%async_computation.25 | async-start | bytes 3145728 | tf_op jit(solution)/shard_map/psum | solution.py:169
  378.0 15.2 %copy-start.47 = (f32[256,768]{1,0:T(8,128)}, f32[256,768]{1,0:T(8,128)S(1)}, u32[]{:S(2)}) copy-start(f32[256,768]{1,0:T(8,128)S(1)} %get-tuple-element.171) | copy-start | bytes 2359300
  378.9 4.6 copy-start.33
  378.9 6.2 copy-start.50
  378.9 10.2 %copy-start.39 = (f32[256,768]{1,0:T(8,128)}, f32[256,768]{1,0:T(8,128)S(1)}, u32[]{:S(2)}) copy-start(f32[256,768]{1,0:T(8,128)S(1)} %get-tuple-element.168) | copy-start | bytes 2359300
  398.1 166.3 %reduce-scatter.31.cloned.1.call-start = ((), (), s32[]{:S(2)}) async-start(), calls=%async_computation.20 | async-start | bytes 1966080
  454.2 4.2 copy-start.15
  454.2 4.2 copy-start.40
  454.2 4.2 copy-start.112
  454.2 4.2 copy-start.113
  454.2 4.2 copy-start.162
  454.3 4.2 copy-start.177
  484.1 81.6 %reduce-scatter.27.cloned.1.call-start = ((), (), s32[]{:S(2)}) async-start(), calls=%async_computation.18 | async-start | bytes 1966080
  508.7 65.3 %reduce-scatter.25.cloned.1.call-start = ((), (), s32[]{:S(2)}) async-start(), calls=%async_computation.17 | async-start | bytes 1966080
  532.5 72.8 %reduce-scatter.29.cloned.1.call-start = ((), (), s32[]{:S(2)}) async-start(), calls=%async_computation.19 | async-start | bytes 1966080
  532.8 4.8 copy-start.8
  551.9 4.5 copy-start.27
  552.0 137.4 %all-reduce.17.cloned.1.call-start = ((), (), s32[]{:S(2)}) async-start(), calls=%async_computation.24 | async-start | bytes 3145728 | tf_op jit(solution)/shard_map/psum | solution.py:219
  562.0 49.2 %copy-start.97 = (bf16[1,256,384]{2,1,0:T(8,128)(2,1)}, bf16[1,256,384]{2,1,0:T(8,128)(2,1)S(1)}, u32[]{:S(2)}) copy-start(bf16[1,256,384]{2,1,0:T(8,128)(2,1)S(1)} %copy.141) | copy-start | bytes 589828
  564.4 50.0 %copy-start.100 = (bf16[1,256,384]{2,1,0:T(8,128)(2,1)}, bf16[1,256,384]{2,1,0:T(8,128)(2,1)S(1)}, u32[]{:S(2)}) copy-start(bf16[1,256,384]{2,1,0:T(8,128)(2,1)S(1)} %copy.155) | copy-start | bytes 589828
  565.7 51.9 %copy-start.61 = (bf16[2,2,128,384]{3,2,1,0:T(8,128)(2,1)}, bf16[2,2,128,384]{3,2,1,0:T(8,128)(2,1)S(1)}, u32[]{:S(2)}) copy-start(bf16[2,2,128,384]{3,2,1,0:T(8,128)(2,1)S(1)} %copy.161) | copy-start | bytes 1179652
  567.0 49.6 %copy-start.63 = (bf16[2,2,128,384]{3,2,1,0:T(8,128)(2,1)}, bf16[2,2,128,384]{3,2,1,0:T(8,128)(2,1)S(1)}, u32[]{:S(2)}) copy-start(bf16[2,2,128,384]{3,2,1,0:T(8,128)(2,1)S(1)} %copy.147) | copy-start | bytes 1179652
  567.0 39.5 %copy-start.110 = (bf16[1,256,384]{2,1,0:T(8,128)(2,1)S(1)}, bf16[1,256,384]{2,1,0:T(8,128)(2,1)}, u32[]{:S(2)}) copy-start(bf16[1,256,384]{2,1,0:T(8,128)(2,1)} %copy.162) | copy-start | bytes 589828
  575.2 40.7 %copy-start.65 = (bf16[2,2,128,384]{3,2,1,0:T(8,128)(2,1)}, bf16[2,2,128,384]{3,2,1,0:T(8,128)(2,1)S(1)}, u32[]{:S(2)}) copy-start(bf16[2,2,128,384]{3,2,1,0:T(8,128)(2,1)S(1)} %copy.140) | copy-start | bytes 1179652
  606.5 7.9 copy-start.67
  614.1 92.8 %reduce-scatter.33.cloned.1.call-start = ((), (), s32[]{:S(2)}) async-start(), calls=%async_computation.21 | async-start | bytes 2211840
  625.1 4.5 copy-start.45
  625.1 4.5 copy-start.107
  625.1 105.8 %reduce-scatter.19.cloned.1.call-start = ((), (), s32[]{:S(2)}) async-start(), calls=%async_computation.14 | async-start | bytes 737280 | tf_op jit(solution)/shard_map/reduce_scatter | solution.py:54
  634.4 145.2 %reduce-scatter.21.cloned.1.call-start = ((), (), s32[]{:S(2)}) async-start(), calls=%async_computation.15 | async-start | bytes 2949120 | tf_op jit(solution)/shard_map/reduce_scatter | solution.py:57
  640.9 188.5 %reduce-scatter.23.cloned.1.call-start = ((), (), s32[]{:S(2)}) async-start(), calls=%async_computation.16 | async-start | bytes 2949120 | tf_op jit(solution)/shard_map/reduce_scatter | solution.py:60
  649.4 232.1 %all-reduce.15.cloned.1.call-start = ((), (), s32[]{:S(2)}) async-start(), calls=%async_computation.23 | async-start | bytes 3833856 | tf_op jit(solution)/shard_map/psum | solution.py:238
  653.8 35.6 %copy-start.46 = (f32[256,768]{1,0:T(8,128)S(1)}, f32[256,768]{1,0:T(8,128)}, u32[]{:S(2)}) copy-start(f32[256,768]{1,0:T(8,128)} %get-tuple-element.139) | copy-start | bytes 2359300
  708.4 121.0 %copy-start.142 = (bf16[256,768]{1,0:T(8,128)(2,1)S(1)}, bf16[256,768]{1,0:T(8,128)(2,1)}, u32[]{:S(2)}) copy-start(bf16[256,768]{1,0:T(8,128)(2,1)} %get-tuple-element.126) | copy-start | bytes 1179652
  881.5 4.2 copy-start.137
  (193 other events, 381.2 us)
Sparse Core Ops, SparseCore 0:
  9.6 43.0 all-gather.6
  55.7 18.6 all-gather.8
  76.0 19.6 all-gather.12
  97.1 19.6 all-gather.16
  118.7 19.6 all-gather.14
  169.6 86.3 all-reduce.12
  257.7 50.4 all-gather.10
  316.6 50.8 all-reduce.20
  398.2 52.0 all-reduce.18
  484.3 28.1 reduce-scatter.30
  515.0 28.1 reduce-scatter.26
  545.8 28.1 reduce-scatter.24
  577.1 28.1 reduce-scatter.28
  614.2 52.0 all-reduce.16
  668.5 38.3 reduce-scatter.32
  709.7 21.0 reduce-scatter.18
  733.1 46.3 reduce-scatter.20
  781.8 47.5 reduce-scatter.22
  832.7 48.6 all-reduce.14
